TPU v7x, 32 devices: a whole 2x2x4 slice. The times are simulated.
32 devices in a mesh: dp: 8 (over z, x), tensor: 4 (over y, core).
Axes of the slice: x: 2, y: 2, z: 4, core: 2. Of those that a mesh axis runs over, the one named last changes fastest.
Arguments:
- tokens: bfloat16 [8192, 768], P(('dp', 'tensor')), may hold values from -6 to 6
- timestep: int32 [8], P('dp'), may hold values from 0 to 999
- block_size: int32 [8], P('dp'), may hold values from 128 to 512, as said below
- table: bfloat16 [1000, 768], replicated, may hold values from -6 to 6
- ln1_gain: bfloat16 [2, 768], replicated, may hold values from 0.5 to 1.5
- ln1_bias: bfloat16 [2, 768], replicated, may hold values from -3 to 3
- w_qkv: bfloat16 [2, 768, 3, 768], P(None, None, None, 'tensor'), may hold values from -0.21875 to 0.21875
- w_out: bfloat16 [2, 768, 768], P(None, 'tensor'), may hold values from -0.875 to 0.875
- b_out: bfloat16 [2, 768], replicated, may hold values from -3 to 3
- ln2_gain: bfloat16 [2, 768], replicated, may hold values from 0.5 to 1.5
- ln2_bias: bfloat16 [2, 768], replicated, may hold values from -3 to 3
- w_up: bfloat16 [2, 768, 3072], P(None, None, 'tensor'), may hold values from -0.21875 to 0.21875
- b_up: bfloat16 [2, 3072], P(None, 'tensor'), may hold values from -3 to 3
- w_down: bfloat16 [2, 3072, 768], P(None, 'tensor'), may hold values from -0.109375 to 0.109375
- b_down: bfloat16 [2, 768], replicated, may hold values from -3 to 3
- cotangent: bfloat16 [8192, 768], P(('dp', 'tensor')), may hold values from -6 to 6
Outputs:
- output: bfloat16 [8192, 768], P(('dp', 'tensor'))
- grad_tokens: float32 [8192, 768], P(('dp', 'tensor'))
- grad_table: float32 [1000, 768], P(None, 'dp')
- grad_ln1_gain: float32 [2, 768], P(None, 'dp')
- grad_ln1_bias: float32 [2, 768], P(None, 'dp')
- grad_w_qkv: float32 [2, 768, 3, 768], P(None, 'dp', None, 'tensor')
- grad_w_out: float32 [2, 768, 768], P(None, 'tensor', 'dp')
- grad_b_out: float32 [2, 768], P(None, 'dp')
- grad_ln2_gain: float32 [2, 768], P(None, 'dp')
- grad_ln2_bias: float32 [2, 768], P(None, 'dp')
- grad_w_up: float32 [2, 768, 3072], P(None, 'dp', 'tensor')
- grad_b_up: float32 [2, 3072], P(None, ('tensor', 'dp'))
- grad_w_down: float32 [2, 3072, 768], P(None, 'tensor', 'dp')
- grad_b_down: float32 [2, 768], P(None, 'dp')
Inputs may be any that keep to these rules, and one draw needn't show every extreme that they name: `block_size`: every sequence's block length is 128, 256 or 512, and all three occur.
All inputs are finite; a program needn't handle non-finite values.
Results may differ from a plain program's by a relative error of at most 0.019.
Values may be sent and summed in bfloat16 or wider, within the bound.
A program may use at most 192 MiB of HBM per device.

v0:
```python
import functools

import jax
import jax.numpy as jnp
from jax import lax
from jax.experimental import pallas as pl
from jax.experimental.pallas import tpu as pltpu
from jax.sharding import PartitionSpec as P

HEAD_DIM = 64
EPSILON = 1e-05
NEGATIVE = -1e30
MESH = pl.DeviceIdType.MESH
BF = jnp.bfloat16
F32 = jnp.float32
INV_SQRT2 = 0.7071067811865476
INV_SQRT2PI = 0.3989422804014327

NN = (((1,), (0,)), ((), ()))
NT = (((1,), (1,)), ((), ()))
TN = (((0,), (0,)), ((), ()))


def mm(a, b, dims=NN):
    return lax.dot_general(a, b, dims, preferred_element_type=F32)


def step_kernel(dim, *refs):
    (
        ts_ref, bs_ref, g1_in, b1_in, bo_in, g2_in, b2_in, bd_in, bup_in,
        tok_in, cot_in, table_h, wqkv_h, wout_h, wup_h, wdown_h,
        out_o, gtok_o, smallx_o, g_o,
        wqkv, wout, wup, wdown, tokf, cotf,
        a_b, a2_b, g_b, gp_b, qkvT, kv_b, oT_b, lse_b, h_b, m_b,
        df_b, dz_b, dh_b, doT_b, dqT_b, dkv_acc,
        ysend, yrecv, csend, crecv, part, s_b, p_b, ds_b, gstage,
        small, smallr, smallx, smallp, emb_b,
        send1, recv1, own1, send2, recv2, fstage,
        wsem, tsem_s, tsem_r, ysem_s, ysem_r, casem_s, casem_r, cpsem_s, cpsem_r,
        lsem, osem, gsem, ssem, x1s, x1r,
        r1s, r1r, r2s, r2r,
    ) = refs
    D, FL, HL, R, L = dim["D"], dim["FL"], dim["HL"], dim["R"], dim["L"]
    N, NI, NO, PER, FUSED = dim["N"], dim["NI"], dim["NO"], dim["PER"], dim["FUSED"]
    HP = HL
    vecs = (g1_in, b1_in, bo_in, g2_in, b2_in, bd_in)

    def vrow(i, l):
        return vecs[i][l : l + 1, :].astype(F32)

    T = 4 * R
    NH = HL // HEAD_DIM
    CH = 2 * R
    NB = D // 256
    FB = FL // 256
    t = lax.axis_index("tensor")
    d = lax.axis_index("dp")
    di = lax.rem(d, NI)
    do_ = lax.div(d, NI)
    y = lax.div(t, 2)
    c = lax.rem(t, 2)
    ypeer = lax.rem(t + 2, 4)
    cpeer = t + 1 - 2 * c

    def own(r):
        return pl.multiple_of(R * (2 * r + c), R)

    def oth(r):
        return pl.multiple_of(R * (2 * r + 1 - c), R)

    def remote(src, dst, ss, rs, peer):
        return pltpu.make_async_remote_copy(
            src_ref=src, dst_ref=dst, send_sem=ss, recv_sem=rs,
            device_id={"tensor": peer}, device_id_type=MESH)

    def dp_remote(src, dst, ss, rs, peer):
        return pltpu.make_async_remote_copy(
            src_ref=src, dst_ref=dst, send_sem=ss, recv_sem=rs,
            device_id={"dp": peer}, device_id_type=MESH)

    bar = pltpu.get_barrier_semaphore()

    def greet(k, cy):
        pl.semaphore_signal(bar, inc=1, device_id={"dp": lax.rem(d + k, N)}, device_id_type=MESH)
        return cy

    lax.fori_loop(1, N, greet, 0)
    pl.semaphore_signal(bar, inc=1, device_id={"tensor": ypeer}, device_id_type=MESH)
    pl.semaphore_signal(bar, inc=1, device_id={"tensor": cpeer}, device_id_type=MESH)

    loc = [pltpu.make_async_copy(tok_in, tokf.at[y], lsem.at[0]),
           pltpu.make_async_copy(cot_in, cotf.at[y], lsem.at[1]),
           pltpu.make_async_copy(table_h, df_b.at[pl.ds(0, dim["TS"]), :], lsem.at[2])]
    for cp in loc:
        cp.start()
    wcopies = []
    for l in range(L):
        row = []
        for i, (src, dst) in enumerate(((wqkv_h, wqkv), (wout_h, wout), (wup_h, wup), (wdown_h, wdown))):
            cp = pltpu.make_async_copy(src.at[l], dst.at[l], wsem.at[l, i])
            cp.start()
            row.append(cp)
        wcopies.append(row)
    pl.semaphore_wait(bar, N + 1)
    tcp = [remote(tok_in, tokf.at[y], tsem_s.at[0], tsem_r.at[0], ypeer),
           remote(cot_in, cotf.at[y], tsem_s.at[1], tsem_r.at[1], ypeer)]
    tcp[0].start()

    small[...] = jnp.zeros_like(small)
    bs = bs_ref[0]
    loc[2].wait()
    pick = (lax.broadcasted_iota(jnp.int32, (8, dim["TS"]), 1) == ts_ref[0]).astype(BF)
    emb_b[...] = mm(pick, df_b[0 : dim["TS"], :])

    def y_copy(par, r):
        return remote(ysend.at[par, r], yrecv.at[par, r], ysem_s.at[par, r], ysem_r.at[par, r], ypeer)

    def tile_copy(buf, r):
        return remote(buf.at[pl.ds(own(r), R), :], buf.at[pl.ds(own(r), R), :],
                      casem_s.at[r], casem_r.at[r], cpeer)

    def part_copy(r):
        return remote(csend.at[r], crecv.at[r], cpsem_s.at[r], cpsem_r.at[r], cpeer)

    BLK = dim["BLK"]

    def rowloop(fn, init=0):
        return lax.fori_loop(0, R // BLK, lambda i, cy: fn(pl.multiple_of(i * BLK, BLK), cy), init)

    def ln_stats(x):
        mean = jnp.sum(x, axis=-1, keepdims=True) * (1.0 / D)
        xc = x - mean
        var = jnp.sum(xc * xc, axis=-1, keepdims=True) * (1.0 / D)
        return xc, lax.rsqrt(var + EPSILON)

    def enter_fwd(l, r, src, gi, dst_h, dst_a):
        gain = vrow(gi, l)
        bias = vrow(gi + 1, l)

        def blk(i, cy):
            x = src(i)
            dst_h[l, r, pl.ds(i, BLK), :] = x
            xc, rstd = ln_stats(x)
            dst_a[l, pl.ds(pl.multiple_of(own(r) + i, BLK), BLK), :] = (xc * rstd * gain + bias).astype(BF)
            return cy

        rowloop(blk)
        cp = tile_copy(dst_a.at[l], r)
        cp.start()
        return cp

    def ysum(par, r, i):
        return ysend[par, r, pl.ds(i, BLK), :].astype(F32) + yrecv[par, r, pl.ds(i, BLK), :].astype(F32)

    def wait_y(par, r):
        cp = y_copy(par, r)
        cp.wait_send()
        cp.wait_recv()

    def send_partner(r, fill):
        fill(csend.at[r])
        cp = part_copy(r)
        cp.start()
        return cp

    def combine(par, r, cp):
        cp.wait_recv()

        def blk(i, cy):
            v = part[pl.ds(i, BLK), :] + crecv[r, pl.ds(i, BLK), :].astype(F32)
            ysend[par, r, pl.ds(i, BLK), :] = v.astype(BF)
            return cy

        rowloop(blk)
        cp.wait_send()
        y_copy(par, r).start()

    def qkv_tile(l, q0):
        q = mm(wqkv[l, 0:HP, :], a_b[l, pl.ds(q0, R), :], NT).astype(BF)
        qkvT[l, 0:HP, pl.ds(q0, R)] = q * jnp.asarray(HEAD_DIM ** -0.5, BF)
        for cc in (1, 2):
            v = mm(wqkv[l, cc * HP : cc * HP + HP, :], a_b[l, pl.ds(q0, R), :], NT)
            qkvT[l, cc * HP : cc * HP + HP, pl.ds(q0, R)] = v.astype(BF)
            kv_b[l, cc - 1, pl.ds(q0, R), :] = v.T.astype(BF)

    def hmask(h):
        rows = lax.broadcasted_iota(jnp.int32, (HP, R), 0)
        return (rows >= h * HEAD_DIM) & (rows < (h + 1) * HEAD_DIM)

    def visible(r, kb, q0):
        key = lax.broadcasted_iota(jnp.int32, (R, R), 0) + (CH * r + kb * R)
        qry = lax.broadcasted_iota(jnp.int32, (R, R), 1) + q0
        return key <= (qry | (bs - 1))

    def att_fwd_tile(l, r, q0):
        KB = 2 * (r + 1)

        def head(h, cy):
            qm = jnp.where(hmask(h), qkvT[l, 0:HP, pl.ds(q0, R)].astype(F32), 0.0).astype(BF)
            top = None
            for kb in range(KB):
                s = mm(kv_b[l, 0, kb * R : kb * R + R, :], qm)
                if kb >= 2 * r:
                    s = jnp.where(visible(r, kb - 2 * r, q0), s, NEGATIVE)
                s_b[kb * R : kb * R + R, :] = s
                mx = jnp.max(s, axis=0, keepdims=True)
                top = mx if top is None else jnp.maximum(top, mx)
            tot = None
            for kb in range(KB):
                e = jnp.exp(s_b[kb * R : kb * R + R, :] - top)
                p_b[kb * R : kb * R + R, :] = e.astype(BF)
                sm = jnp.sum(e, axis=0, keepdims=True)
                tot = sm if tot is None else tot + sm
            hr = pl.multiple_of(h * HEAD_DIM, HEAD_DIM)
            o = mm(qkvT[l, pl.ds(pl.multiple_of(2 * HP + hr, HEAD_DIM), HEAD_DIM), 0 : KB * R], p_b[0 : KB * R, :])
            oT_b[l, pl.ds(hr, HEAD_DIM), pl.ds(q0, R)] = (o * (1.0 / tot)).astype(BF)
            lse_b[l, pl.ds(h, 1), pl.ds(q0, R)] = top + jnp.log(tot)
            return cy

        lax.fori_loop(0, NH, head, 0)

    def nblocks(fn, n):
        for i in range(n):
            fn(i * 256)

    def out_tile(l, q0, dst):
        o = oT_b[l, :, pl.ds(q0, R)].astype(F32).T.astype(BF)

        def one(n):
            dst[:, n : n + 256] = mm(o, wout[l, :, n : n + 256]).astype(dst.dtype)

        nblocks(one, NB)

    def up_tile(l, q0):
        def one(n, cy):
            n = pl.multiple_of(n * 256, 256)
            u = mm(a2_b[l, pl.ds(q0, R), :], wup[l, :, pl.ds(n, 256)]) + bup_in[l : l + 1, pl.ds(n, 256)].astype(F32)
            phi = 0.5 * (1.0 + lax.erf(u * INV_SQRT2))
            g_b[l, pl.ds(q0, R), pl.ds(n, 256)] = (u * phi).astype(BF)
            gp = phi + u * (jnp.exp(u * u * -0.5) * INV_SQRT2PI)
            gp_b[l, pl.ds(q0, R), pl.ds(n, 256)] = gp.astype(BF)
            return cy

        lax.fori_loop(0, FB, one, 0)

    def down_tile(l, q0, dst):
        def one(n):
            dst[:, n : n + 256] = mm(g_b[l, pl.ds(q0, R), :], wdown[l, :, n : n + 256]).astype(dst.dtype)

        nblocks(one, NB)

    def own_first(r, tile_cp, fn):
        def tile(i, cy):
            @pl.when(i == 1)
            def _():
                tile_cp.wait_recv()

            fn(pl.multiple_of(R * (2 * r + c + i * (1 - 2 * c)), R))
            return cy

        lax.fori_loop(0, 2, tile, 0)

    def att_fwd(l, r, tile_cp):
        own_first(r, tile_cp, lambda q0: qkv_tile(l, q0))
        cp = part_copy(r)

        def tile(i, cy):
            att_fwd_tile(l, r, pl.multiple_of(R * (2 * r + 1 - c + i * (2 * c - 1)), R))

            @pl.when(i == 0)
            def _():
                out_tile(l, oth(r), csend.at[r])
                cp.start()

            return cy

        lax.fori_loop(0, 2, tile, 0)
        out_tile(l, own(r), part)
        tile_cp.wait_send()
        combine(0, r, cp)

    def ffn_fwd(l, r, tile_cp):
        own_first(r, tile_cp, lambda q0: up_tile(l, q0))
        cp = send_partner(r, lambda ref: down_tile(l, oth(r), ref))
        down_tile(l, own(r), part)
        tile_cp.wait_send()
        combine(1, r, cp)

    for l in range(L):
        for r in range(2):
            if l == 0:
                if r == 0:
                    for cp in (loc[0], wcopies[0][0]):
                        cp.wait()
                    tcp[0].wait()
                    tcp[1].start()
                src = lambda i, r=r: tokf[r, pl.ds(i, BLK), :].astype(F32) + emb_b[0:1, :]
            else:
                wait_y(1, r)
                bd = vrow(5, l - 1)
                src = lambda i, r=r, l=l, bd=bd: m_b[l - 1, r, pl.ds(i, BLK), :] + (ysum(1, r, i) + bd)
            if r == 0 and l > 0:
                wcopies[l][0].wait()
            cp = enter_fwd(l, r, src, 0, h_b, a_b)
            if r == 0:
                wcopies[l][1].wait()
            att_fwd(l, r, cp)
        for r in range(2):
            wait_y(0, r)
            bo = vrow(2, l)
            src = lambda i, r=r, l=l, bo=bo: h_b[l, r, pl.ds(i, BLK), :] + (ysum(0, r, i) + bo)
            if r == 0:
                wcopies[l][2].wait()
                wcopies[l][3].wait()
            cp = enter_fwd(l, r, src, 3, m_b, a2_b)
            ffn_fwd(l, r, cp)

    def finish_output(r):
        wait_y(1, r)
        bd = vrow(5, L - 1)

        def blk(i, cy):
            v = m_b[L - 1, r, pl.ds(i, BLK), :] + (ysum(1, r, i) + bd)
            tokf[r, pl.ds(i, BLK), :] = v.astype(BF)
            return cy

        rowloop(blk)

    def ln_bwd(l, r, par, gi, xbuf, emit):
        gain = vrow(gi, l)

        def blk(i, cy):
            dg, db = cy
            x = xbuf[l, r, pl.ds(i, BLK), :]
            dy = ysum(par, r, i)
            xc, rstd = ln_stats(x)
            xh = xc * rstd
            t1 = dy * gain
            m1 = jnp.sum(t1, axis=-1, keepdims=True) * (1.0 / D)
            m2 = jnp.sum(t1 * xh, axis=-1, keepdims=True) * (1.0 / D)
            dx = rstd * (t1 - m1 - xh * m2)
            emit(i, dx)
            dg = dg + jnp.sum(dy * xh, axis=0, keepdims=True)
            db = db + jnp.sum(dy, axis=0, keepdims=True)
            return (dg, db)

        z = jnp.zeros((1, D), F32)
        dg, db = rowloop(blk, (z, z))
        small[l, gi : gi + 1, :] = small[l, gi : gi + 1, :] + dg
        small[l, gi + 1 : gi + 2, :] = small[l, gi + 1 : gi + 2, :] + db

    def colsum_own(buf, r, l, row):
        def blk(i, cy):
            return cy + jnp.sum(buf[pl.ds(pl.multiple_of(own(r) + i, BLK), BLK), :].astype(F32), axis=0, keepdims=True)

        v = rowloop(blk, jnp.zeros((1, D), F32))
        small[l, row : row + 1, :] = small[l, row : row + 1, :] + v

    def enter_b1(l, r):
        if l == L - 1:
            def blk(i, cy):
                v = cotf[r, pl.ds(i, BLK), :]
                dh_b[r, pl.ds(i, BLK), :] = v.astype(F32)
                df_b[pl.ds(pl.multiple_of(own(r) + i, BLK), BLK), :] = v
                return cy

            rowloop(blk)
        else:
            wait_y(0, r)

            def emit(i, dx):
                v = dh_b[r, pl.ds(i, BLK), :] + dx
                dh_b[r, pl.ds(i, BLK), :] = v
                df_b[pl.ds(pl.multiple_of(own(r) + i, BLK), BLK), :] = v.astype(BF)

            ln_bwd(l + 1, r, 0, 0, h_b, emit)
        cp = tile_copy(df_b, r)
        cp.start()
        colsum_own(df_b, r, l, 5)
        return cp

    def du_tile(l, q0):
        def one(n, cy):
            n = pl.multiple_of(n * 256, 256)
            dg = mm(df_b[pl.ds(q0, R), :], wdown[l, pl.ds(n, 256), :], NT)
            du = (dg * gp_b[l, pl.ds(q0, R), pl.ds(n, 256)].astype(F32)).astype(BF)
            gp_b[l, pl.ds(q0, R), pl.ds(n, 256)] = du
            small[l, 7:8, pl.ds(n, 256)] = small[l, 7:8, pl.ds(n, 256)] + jnp.sum(du.astype(F32), axis=0, keepdims=True)
            return cy

        lax.fori_loop(0, FB, one, 0)

    def da2_tile(l, q0, dst):
        def one(n):
            dst[:, n : n + 256] = mm(gp_b[l, pl.ds(q0, R), :], wup[l, n : n + 256, :], NT).astype(dst.dtype)

        nblocks(one, NB)

    def ffn_bwd(l, r, tile_cp):
        own_first(r, tile_cp, lambda q0: du_tile(l, q0))
        cp = send_partner(r, lambda ref: da2_tile(l, oth(r), ref))
        da2_tile(l, own(r), part)
        tile_cp.wait_send()
        combine(2, r, cp)

    def enter_b2(l, r):
        wait_y(2, r)

        def emit(i, dx):
            v = dh_b[r, pl.ds(i, BLK), :] + dx
            dh_b[r, pl.ds(i, BLK), :] = v
            dz_b[pl.ds(pl.multiple_of(own(r) + i, BLK), BLK), :] = v.astype(BF)

        ln_bwd(l, r, 2, 3, m_b, emit)
        cp = tile_copy(dz_b, r)
        cp.start()
        colsum_own(dz_b, r, l, 2)
        return cp

    def do_tile(l, q0):
        doT_b[:, pl.ds(q0, R)] = mm(wout[l], dz_b[pl.ds(q0, R), :], NT).astype(BF)

    def att_bwd_tile(l, r, q0):
        KB = 2 * (r + 1)
        KN = KB * R

        def head(h, cy):
            hr = pl.multiple_of(h * HEAD_DIM, HEAD_DIM)
            hm = hmask(h)
            qm = jnp.where(hm, qkvT[l, 0:HP, pl.ds(q0, R)].astype(F32), 0.0).astype(BF)
            dom = jnp.where(hm, doT_b[:, pl.ds(q0, R)].astype(F32), 0.0).astype(BF)
            do_h = doT_b[pl.ds(hr, HEAD_DIM), pl.ds(q0, R)]
            q_h = qkvT[l, pl.ds(hr, HEAD_DIM), pl.ds(q0, R)]
            o_h = oT_b[l, pl.ds(hr, HEAD_DIM), pl.ds(q0, R)]
            dsum = jnp.sum(do_h.astype(F32) * o_h.astype(F32), axis=0, keepdims=True)
            lse = lse_b[l, pl.ds(h, 1), pl.ds(q0, R)]
            for kb in range(KB):
                ks = slice(kb * R, kb * R + R)
                s = mm(kv_b[l, 0, ks, :], qm)
                p = jnp.exp(s - lse)
                if kb >= 2 * r:
                    p = jnp.where(visible(r, kb - 2 * r, q0), p, 0.0)
                p_b[ks, :] = p.astype(BF)
                dp = mm(kv_b[l, 1, ks, :], dom)
                ds_b[ks, :] = (p * (dp - dsum)).astype(BF)
            dkv_acc[1, pl.ds(hr, HEAD_DIM), 0:KN] = dkv_acc[1, pl.ds(hr, HEAD_DIM), 0:KN] + mm(do_h, p_b[0:KN, :], NT)
            dkv_acc[0, pl.ds(hr, HEAD_DIM), 0:KN] = dkv_acc[0, pl.ds(hr, HEAD_DIM), 0:KN] + mm(q_h, ds_b[0:KN, :], NT)
            k_h = qkvT[l, pl.ds(pl.multiple_of(HP + hr, HEAD_DIM), HEAD_DIM), 0:KN]
            dq = mm(k_h, ds_b[0:KN, :]) * (HEAD_DIM ** -0.5)
            dqT_b[pl.ds(hr, HEAD_DIM), pl.ds(q0, R)] = dq.astype(BF)
            return cy

        lax.fori_loop(0, NH, head, 0)

    def da_tile(l, q0, dst):
        dqkv = dqT_b[:, pl.ds(q0, R)].astype(F32).T.astype(BF)

        def one(n):
            dst[:, n : n + 256] = mm(dqkv, wqkv[l, :, n : n + 256]).astype(dst.dtype)

        nblocks(one, NB)

    def att_bwd(l, r, tile_cp):
        def both(q0):
            do_tile(l, q0)
            att_bwd_tile(l, r, q0)

        own_first(r, tile_cp, both)
        cs = slice(CH * r, CH * r + CH)
        for j in range(2):
            dqT_b[HP * (j + 1) : HP * (j + 1) + HL, cs] = dkv_acc[j, 0:HL, cs].astype(BF)
        cp = send_partner(r, lambda ref: da_tile(l, oth(r), ref))
        da_tile(l, own(r), part)
        tile_cp.wait_send()
        combine(0, r, cp)

    WHOLE = (0, FL, None)
    HALF = ((0, FL // 2, None), (FL // 2, FL - FL // 2, 3))

    def r1_copy(j, k, span):
        c0, w, extra = span
        q = j if extra is None else extra
        peer = do_ * NI + lax.rem(di + k, NI)
        return dp_remote(send1.at[j, k - 1, :, c0 : c0 + w], recv1.at[j, k - 1, :, c0 : c0 + w],
                         r1s.at[q, k - 1], r1r.at[q, k - 1], peer)

    def r2_copy(j, k, span):
        c0, w, extra = span
        q = j if extra is None else extra
        peer = lax.rem(do_ + k, NO) * NI + di
        return dp_remote(send2.at[j, k - 1, :, c0 : c0 + w], recv2.at[j, k - 1, :, c0 : c0 + w],
                         r2s.at[q, k - 1], r2r.at[q, k - 1], peer)

    def g_copy(l, j, span):
        c0, w, extra = span
        q = l * 3 + j if extra is None else 3 * L
        return pltpu.make_async_copy(fstage.at[l, j, :, c0 : c0 + w], g_o.at[l, j, :, c0 : c0 + w], gsem.at[q])

    def piece(q):
        return pl.ds(pl.multiple_of(q * PER, PER), PER)

    def rs_start(l, j, span=WHOLE):
        c0, w, _ = span
        cols = slice(c0, c0 + w)
        if not FUSED:
            cp = pltpu.make_async_copy(gstage.at[:, cols], g_o.at[l, j, :, cols], gsem.at[0])
            cp.start()
            cp.wait()
            return
        for k in range(1, NI):
            for oo in range(NO):
                send1[j, k - 1, oo * PER : oo * PER + PER, cols] = gstage[piece(oo * NI + lax.rem(di + k, NI)), cols].astype(BF)
            r1_copy(j, k, span).start()
        for oo in range(NO):
            own1[j, oo * PER : oo * PER + PER, cols] = gstage[piece(oo * NI + di), cols]

    def rs_mid(l, j, span=WHOLE):
        c0, w, _ = span
        cols = slice(c0, c0 + w)
        if not FUSED:
            return
        for k in range(1, NI):
            cp = r1_copy(j, k, span)
            cp.wait_send()
            cp.wait_recv()
        for kk in range(NO - 1, -1, -1):
            rows = piece(lax.rem(do_ + kk, NO))
            v = own1[j, rows, cols]
            for k in range(1, NI):
                v = v + recv1[j, k - 1, rows, cols].astype(F32)
            if kk == 0:
                own1[j, rows, cols] = v
            else:
                send2[j, kk - 1, :, cols] = v.astype(BF)
                r2_copy(j, kk, span).start()

    def rs_fin(l, j, span=WHOLE):
        c0, w, _ = span
        cols = slice(c0, c0 + w)
        if not FUSED:
            return
        v = own1[j, piece(do_), cols]
        for kk in range(1, NO):
            cp = r2_copy(j, kk, span)
            cp.wait_send()
            cp.wait_recv()
            v = v + recv2[j, kk - 1, :, cols].astype(F32)
        fstage[l, j, :, cols] = v
        g_copy(l, j, span).start()

    def wgrad_ffn(l, j, lhs, rhs):
        def one(n, cy):
            ns = pl.ds(pl.multiple_of(n * 256, 256), 256)
            lt = lhs[:, ns].astype(F32).T.astype(BF)
            for f in range(FB):
                gstage[ns, f * 256 : f * 256 + 256] = mm(lt, rhs[:, f * 256 : f * 256 + 256])
            return cy

        lax.fori_loop(0, NB, one, 0)

    def wgrad_att(l, span):
        lo, hi = span[0], span[0] + span[1]
        q = min(hi, 3 * HL)

        def one(n, cy):
            ns = pl.ds(pl.multiple_of(n * 256, 256), 256)
            s_b[lo:q, :] = mm(dqT_b[lo:q, :], a_b[l, :, ns])
            if hi > q:
                s_b[q:hi, :] = mm(oT_b[l], dz_b[:, ns])
            gstage[ns, lo:hi] = s_b[lo:hi, :].T
            return cy

        lax.fori_loop(0, NB, one, 0)

    loc[1].wait()
    tcp[1].wait()
    for l in range(L - 1, -1, -1):
        last = l == L - 1
        if last:
            cps = {r: enter_b1(l, r) for r in (1, 0)}
        for r in (1, 0):
            cp = cps[r] if last else enter_b1(l, r)
            ffn_bwd(l, r, cp)
            if not last:
                rs_fin(l + 1, 1 + r)
        if last:
            for r in (1, 0):
                finish_output(r)
        else:
            rs_mid(l + 1, 0)
        wgrad_ffn(l, 2, df_b, g_b.at[l])
        rs_start(l, 2)
        wgrad_ffn(l, 1, a2_b.at[l], gp_b.at[l])
        rs_start(l, 1)
        dkv_acc[...] = jnp.zeros_like(dkv_acc)
        for r in (1, 0):
            cp = enter_b2(l, r)
            att_bwd(l, r, cp)
            if r == 1:
                if not last:
                    rs_fin(l + 1, 0)
                rs_mid(l, 2)
        if l > 0:
            wgrad_att(l, WHOLE)
            rs_mid(l, 1)
            rs_start(l, 0)
        else:
            wgrad_att(l, HALF[0])
            rs_mid(l, 1)
            rs_start(l, 0, HALF[0])
            wgrad_att(l, HALF[1])
            rs_start(l, 0, HALF[1])
    ocp = pltpu.make_async_copy(tokf.at[y], out_o, osem.at[0])
    ocp.start()
    rs_fin(0, 2)
    for r in (1, 0):
        wait_y(0, r)

        def emit(i, dx, r=r):
            v = dh_b[r, pl.ds(i, BLK), :] + dx
            dh_b[r, pl.ds(i, BLK), :] = v
            small[0, 6:7, :] = small[0, 6:7, :] + jnp.sum(v, axis=0, keepdims=True)

        ln_bwd(0, r, 0, 0, h_b, emit)
        if r == 1:
            rs_mid(0, 0, HALF[0])
    gcp = pltpu.make_async_copy(dh_b.at[y], gtok_o, osem.at[1])
    gcp.start()
    scp = remote(small, smallr, ssem.at[0], ssem.at[1], cpeer)
    scp.start()
    rs_fin(0, 1)
    scp.wait()
    shared = lax.broadcasted_iota(jnp.int32, (8, D), 0) < 7
    for l in range(L):
        small[l] = small[l] + jnp.where(shared, smallr[l], 0.0)
    small[1, 6:7, :] = jnp.full((1, D), ts_ref[0].astype(F32), F32)

    def x_copy(k):
        return dp_remote(smallp.at[k], smallx.at[d], x1s.at[k], x1r.at[k], lax.rem(d + k, N))

    def columns(k):
        turn = lax.rem(D - PER * lax.rem(d + k, N), D)
        return [pltpu.roll(small[l], turn, 1)[:, 0 : smallx.shape[3]] for l in range(L)]

    def x_go(k, cy):
        for l, v in enumerate(columns(k)):
            smallp[k, l] = v
        x_copy(k).start()
        return cy

    def x_wait(k, cy):
        cp = x_copy(k)
        cp.wait_send()
        cp.wait_recv()
        return cy

    lax.fori_loop(1, N, x_go, 0)
    for l, v in enumerate(columns(0)):
        smallx[d, l] = v
    rs_mid(0, 0, HALF[1])
    rs_fin(0, 0, HALF[0])
    lax.fori_loop(1, N, x_wait, 0)
    smallx_o[...] = smallx[...]
    rs_fin(0, 0, HALF[1])
    ocp.wait()
    gcp.wait()
    if FUSED:
        for l in range(L):
            for j in range(3):
                for span in HALF if l == 0 and j == 0 else (WHOLE,):
                    g_copy(l, j, span).wait()


def finish_kernel(dim, out_i, gtok_i, sx, g_i, out_o, gtok_o, table_o, dg1, db1, gq, go, dbo, dg2, db2, gup, dbup, gdown, dbd,
                  g_b, out_b, gtok_b, rows_b, sem_i, sem_o):
    FL, HL, L, PER, N, TS = dim["FL"], dim["HL"], dim["L"], dim["PER"], dim["N"], dim["TS"]
    ins = []
    for j in range(3):
        for l in range(L):
            ins.append(pltpu.make_async_copy(g_i.at[l, j], g_b.at[l, j], sem_i.at[l * 3 + j]))
    order = ((out_i, out_b, out_o), (gtok_i, gtok_b, gtok_o))
    for i, (src, buf, _) in enumerate(order):
        ins.append(pltpu.make_async_copy(src, buf, sem_i.at[3 * L + i]))
    for cp in ins:
        cp.start()
    for l in range(L):
        tot = sx[0, l]
        for q in range(1, N):
            tot = tot + sx[q, l]
        for i, ref in enumerate((dg1, db1, dbo, dg2, db2, dbd)):
            ref[l : l + 1, :] = tot[i : i + 1, 0:PER]
        dbup[l : l + 1, :] = tot[7:8, 0:PER]
    for q in range(N):
        rows_b[0, q : q + 1, :] = sx[q, 0, 6:7, :]
        rows_b[1, q : q + 1, :] = sx[q, 1, 6:7, :]
    step = rows_b[1, :, 0:1]
    pick = jnp.where(lax.broadcasted_iota(jnp.int32, (N, TS), 1).astype(F32) == step, 1.0, 0.0)
    table_o[...] = lax.dot_general(rows_b[0], pick, TN, precision=lax.Precision.HIGHEST, preferred_element_type=F32)[0:PER, :]
    for l in range(L):
        ins[l].wait()
        ga = g_b[l, 0]
        for cc in range(3):
            gq[l, cc] = ga[:, cc * HL : cc * HL + HL]
        gt = jnp.concatenate([ga, jnp.zeros((-PER % 128, 4 * HL), F32)], axis=0).T
        go[l] = gt[3 * HL : 4 * HL, 0:PER]
    outs = []
    for j, ref in ((1, gup), (2, gdown)):
        for l in range(L):
            ins[j * L + l].wait()
            cp = pltpu.make_async_copy(g_b.at[l, j], ref.at[l], sem_o.at[l * 2 + j - 1])
            cp.start()
            outs.append(cp)
    for i, (_, buf, dst) in enumerate(order):
        ins[3 * L + i].wait()
        cp = pltpu.make_async_copy(buf, dst, sem_o.at[2 * L + i])
        cp.start()
        outs.append(cp)
    for cp in outs:
        cp.wait()


def split_of(n):
    inner = 2 ** ((n.bit_length() - 1) // 2)
    return inner, n // inner


def run_step(ts, bs, vecs, bup, tok, cot, table, wqkv, wout, wup, wdown):
    R, D = tok.shape
    L, _, FL = wup.shape
    HL = wout.shape[1]
    N = lax.axis_size("dp")
    NI, NO = split_of(N)
    PER = D // N
    FUSED = PER % 16 == 0
    assert lax.axis_size("tensor") == 4 and ts.shape[0] == 1 and FL == D == 4 * HL and L > 1 and R == 256
    T = 4 * R
    W = -(-PER // 128) * 128
    dim = dict(D=D, FL=FL, HL=HL, R=R, L=L, BLK=min(R, 128), W=W, N=N, NI=NI, NO=NO, PER=PER, FUSED=FUSED, TS=table.shape[0])
    vm = pl.BlockSpec(memory_space=pltpu.VMEM)
    sm = pl.BlockSpec(memory_space=pltpu.SMEM)
    any_ = pl.BlockSpec(memory_space=pl.ANY)
    dma = pltpu.SemaphoreType.DMA
    V = pltpu.VMEM
    J = 3 if FUSED else 1
    PR = PER if FUSED else 16
    ones = max(NI - 1, 1)
    outs = max(NO - 1, 1)
    kept = (L, 3, PER, FL) if FUSED else (L, 3, D, FL)
    return dim, pl.pallas_call(
        functools.partial(step_kernel, dim),
        out_shape=(
            jax.ShapeDtypeStruct((R, D), BF),
            jax.ShapeDtypeStruct((R, D), F32),
            jax.ShapeDtypeStruct((N, L, 8, W), F32),
            jax.ShapeDtypeStruct(kept, F32),
        ),
        in_specs=[sm, sm] + [vm] * 7 + [any_] * 7,
        out_specs=(any_, any_, vm, any_),
        scratch_shapes=[
            V((L, 3 * HL, D), BF), V((L, HL, D), BF), V((L, D, FL), BF), V((L, FL, D), BF),
            V((2, R, D), BF), V((2, R, D), BF),
            V((L, T, D), BF), V((L, T, D), BF), V((L, T, FL), BF), V((L, T, FL), BF),
            V((L, 3 * HL, T), BF), V((L, 2, T, HL), BF), V((L, HL, T), BF), V((L, 8, T), F32),
            V((L, 2, R, D), F32), V((L, 2, R, D), F32),
            V((T, D), BF), V((T, D), BF), V((2, R, D), F32),
            V((HL, T), BF), V((3 * HL, T), BF), V((2, HL, T), F32),
            V((3, 2, R, D), BF), V((3, 2, R, D), BF), V((2, R, D), BF), V((2, R, D), BF),
            V((R, D), F32), V((T, R), F32), V((T, R), BF), V((T, R), BF), V((D, FL), F32),
            V((L, 8, D), F32), V((L, 8, D), F32), V((N, L, 8, W), F32), V((N, L, 8, W), F32), V((8, D), F32),
            V((J, ones, NO * PR, FL), BF), V((J, ones, NO * PR, FL), BF), V((J, NO * PR, FL), F32),
            V((J, outs, PR, FL), BF), V((J, outs, PR, FL), BF), V((L, J, PR, FL), F32),
            dma((L, 4)), dma((2,)), dma((2,)), dma((3, 2)), dma((3, 2)),
            dma((2,)), dma((2,)), dma((2,)), dma((2,)),
            dma((3,)), dma((2,)), dma((3 * L + 1,)), dma((2,)), dma((N,)), dma((N,)),
            dma((4, ones)), dma((4, ones)), dma((4, outs)), dma((4, outs)),
        ],
        compiler_params=pltpu.CompilerParams(
            collective_id=0, has_side_effects=True, vmem_limit_bytes=67043328),
        name="layers",
    )(ts, bs, *vecs, bup, tok, cot, table, wqkv, wout, wup, wdown)


def local(tokens, timestep, block_size, table, ln1_gain, ln1_bias, w_qkv, w_out, b_out,
          ln2_gain, ln2_bias, w_up, b_up, w_down, b_down, cotangent):
    L, D, _, HL = w_qkv.shape
    wq = jnp.transpose(w_qkv, (0, 2, 3, 1)).reshape(L, 3 * HL, D)
    vecs = (ln1_gain, ln1_bias, b_out, ln2_gain, ln2_bias, b_down)
    dim, (out, gtok, sx, g) = run_step(
        timestep, block_size, vecs, b_up, tokens, cotangent, table, wq, w_out, w_up, w_down)
    PER, FL, TS = dim["PER"], dim["FL"], dim["TS"]
    if not dim["FUSED"]:
        g = lax.psum_scatter(g, "dp", scatter_dimension=2, tiled=True)
    vec = jax.ShapeDtypeStruct((L, PER), F32)
    big = jax.ShapeDtypeStruct((L, PER, FL), F32)
    vm = pl.BlockSpec(memory_space=pltpu.VMEM)
    any_ = pl.BlockSpec(memory_space=pl.ANY)
    N, W = dim["N"], dim["W"]
    got = pl.pallas_call(
        functools.partial(finish_kernel, dim),
        out_shape=(
            jax.ShapeDtypeStruct(out.shape, BF), jax.ShapeDtypeStruct(gtok.shape, F32),
            jax.ShapeDtypeStruct((PER, TS), F32), vec, vec,
            jax.ShapeDtypeStruct((L, 3, PER, HL), F32), jax.ShapeDtypeStruct((L, HL, PER), F32),
            vec, vec, vec, big, vec, big, vec),
        in_specs=[any_, any_, vm, any_],
        out_specs=(any_, any_) + (vm,) * 8 + (any_, vm, any_, vm),
        scratch_shapes=[
            pltpu.VMEM((L, 3, PER, FL), F32), pltpu.VMEM(out.shape, BF), pltpu.VMEM(gtok.shape, F32),
            pltpu.VMEM((2, N, W), F32), pltpu.SemaphoreType.DMA((3 * L + 2,)), pltpu.SemaphoreType.DMA((2 * L + 2,))],
        name="finish",
    )(out, gtok, sx, g)
    got = list(got)
    got[2] = jnp.transpose(got[2])
    got[5] = jnp.transpose(got[5], (0, 2, 1, 3))
    got[12] = jnp.transpose(got[12], (0, 2, 1))
    return tuple(got)


def solution(mesh):
    placed = (
        P(("dp", "tensor"), None), P("dp"), P("dp"), P(), P(), P(),
        P(None, None, None, "tensor"), P(None, "tensor", None), P(), P(), P(),
        P(None, None, "tensor"), P(None, "tensor"), P(None, "tensor", None), P(),
        P(("dp", "tensor"), None),
    )
    return jax.shard_map(
        local,
        mesh=mesh,
        in_specs=placed,
        out_specs=(
            P(("dp", "tensor"), None), P(("dp", "tensor"), None), P(None, "dp"), P(None, "dp"), P(None, "dp"),
            P(None, "dp", None, "tensor"), P(None, "tensor", "dp"), P(None, "dp"), P(None, "dp"), P(None, "dp"),
            P(None, "dp", "tensor"), P(None, ("tensor", "dp")), P(None, "tensor", "dp"), P(None, "dp"),
        ),
        check_vma=False,
    )
```

profile of v0, /device:TPU:0, one launch (start us, length us, event | category | flops | bytes accessed | tf_op | source)
XLA Modules:
  0.0 206.4 jit_solution(13362348422847955862)
XLA Ops:
  1.9 199.6 %layers.1 = (bf16[256,768]{1,0:T(8,128)(2,1)}, f32[256,768]{1,0:T(8,128)}, f32[8,2,8,128]{3,2,1,0:T(8,128)}, f32[2,3,96,768]{3,2,1,0:T(8,128)}) custom-call(s32[1]{0:T(128)S(6)} %copy.30.refs_0_, s32[1]{0:T(128)S(6)} %copy.31.refs_1_, bf16[2,768]{1,0:T(2,128)(2,1)} %refs_2_.1, bf16[2,768]{1,0:T(2,128)(2,1)} %refs_3_.1, bf16[2,768]{1,0:T(2,128)(2,1)} %refs_4_.1, ...), custom_call_target="tpu_custom_call" | custom-call | tf_op jit(solution)/shard_map/layers/pallas_call | solution.py:749
  201.6 4.7 %finish.1 = (bf16[256,768]{1,0:T(8,128)(2,1)}, f32[256,768]{1,0:T(8,128)}, f32[96,1000]{1,0:T(8,128)}, f32[2,96]{1,0:T(2,128)}, f32[2,96]{1,0:T(2,128)}, /*index...) custom-call(bf16[256,768]{1,0:T(8,128)(2,1)} %get-tuple-element.32.o, ...), custom_call_target="tpu_custom_call" | custom-call | tf_op jit(solution)/shard_map/finish/pallas_call | solution.py:798
where the time goes:
time: 207 us; the launch traced here: 206 us
  Pallas kernels  204 us (99%)
  between operations  2.13 us (1%)
    pallas_call x1, Pallas kernels, run_step(): pl.pallas_call(functools.partial(step_kernel, dim), out_shape=(jax.ShapeD...  200 us
    pallas_call x1, Pallas kernels, local(): pl.pallas_call(functools.partial(finish_kernel, dim), out_shape=(jax.Shap...  4.67 us

commit v1 on v0

--- a/solution.py
+++ b/solution.py
@@ -38,7 +38,7 @@
         send1, recv1, own1, send2, recv2, fstage,
         wsem, tsem_s, tsem_r, ysem_s, ysem_r, casem_s, casem_r, cpsem_s, cpsem_r,
         lsem, osem, gsem, ssem, x1s, x1r,
-        r1s, r1r, r2s, r2r,
+        r1s, r1r, r2s, r2r, turned,
     ) = refs
     D, FL, HL, R, L = dim["D"], dim["FL"], dim["HL"], dim["R"], dim["L"]
     N, NI, NO, PER, FUSED = dim["N"], dim["NI"], dim["NO"], dim["PER"], dim["FUSED"]
@@ -112,12 +112,28 @@
     pick = (lax.broadcasted_iota(jnp.int32, (8, dim["TS"]), 1) == ts_ref[0]).astype(BF)
     emb_b[...] = mm(pick, df_b[0 : dim["TS"], :])
 
-    def y_copy(par, r):
-        return remote(ysend.at[par, r], yrecv.at[par, r], ysem_s.at[par, r], ysem_r.at[par, r], ypeer)
-
-    def tile_copy(buf, r):
-        return remote(buf.at[pl.ds(own(r), R), :], buf.at[pl.ds(own(r), R), :],
-                      casem_s.at[r], casem_r.at[r], cpeer)
+    def y_copy(par, r, i):
+        rows = pl.ds(i, BLK)
+        b = i // BLK
+        return remote(ysend.at[par, r, rows, :], yrecv.at[par, r, rows, :],
+                      ysem_s.at[par, r, b], ysem_r.at[par, r, b], ypeer)
+
+    def tile_copy(buf, r, i, q):
+        rows = pl.ds(pl.multiple_of(own(r) + i, BLK), BLK)
+        b = i // BLK
+        return remote(buf.at[rows, :], buf.at[rows, :], casem_s.at[q, b], casem_r.at[q, b], cpeer)
+
+    class Tile:
+        def __init__(self, buf, r, q=None):
+            self.copy = lambda i: tile_copy(buf, r, i, r if q is None else q)
+
+        def wait_recv(self):
+            for i in range(0, R, BLK):
+                self.copy(i).wait_recv()
+
+        def wait_send(self):
+            for i in range(0, R, BLK):
+                self.copy(i).wait_send()
 
     def part_copy(r):
         return remote(csend.at[r], crecv.at[r], cpsem_s.at[r], cpsem_r.at[r], cpeer)
@@ -133,27 +149,29 @@
         var = jnp.sum(xc * xc, axis=-1, keepdims=True) * (1.0 / D)
         return xc, lax.rsqrt(var + EPSILON)
 
-    def enter_fwd(l, r, src, gi, dst_h, dst_a):
+    def enter_fwd(l, r, src, gi, dst_h, dst_a, par=None):
         gain = vrow(gi, l)
         bias = vrow(gi + 1, l)
+        cp = Tile(dst_a.at[l], r)
 
         def blk(i, cy):
+            if par is not None:
+                wait_y(par, r, i)
             x = src(i)
             dst_h[l, r, pl.ds(i, BLK), :] = x
             xc, rstd = ln_stats(x)
             dst_a[l, pl.ds(pl.multiple_of(own(r) + i, BLK), BLK), :] = (xc * rstd * gain + bias).astype(BF)
+            cp.copy(i).start()
             return cy
 
         rowloop(blk)
-        cp = tile_copy(dst_a.at[l], r)
-        cp.start()
         return cp
 
     def ysum(par, r, i):
         return ysend[par, r, pl.ds(i, BLK), :].astype(F32) + yrecv[par, r, pl.ds(i, BLK), :].astype(F32)
 
-    def wait_y(par, r):
-        cp = y_copy(par, r)
+    def wait_y(par, r, i):
+        cp = y_copy(par, r, i)
         cp.wait_send()
         cp.wait_recv()
 
@@ -169,11 +187,11 @@
         def blk(i, cy):
             v = part[pl.ds(i, BLK), :] + crecv[r, pl.ds(i, BLK), :].astype(F32)
             ysend[par, r, pl.ds(i, BLK), :] = v.astype(BF)
+            y_copy(par, r, i).start()
             return cy
 
         rowloop(blk)
         cp.wait_send()
-        y_copy(par, r).start()
 
     def qkv_tile(l, q0):
         q = mm(wqkv[l, 0:HP, :], a_b[l, pl.ds(q0, R), :], NT).astype(BF)
@@ -251,9 +269,10 @@
 
     def own_first(r, tile_cp, fn):
         def tile(i, cy):
-            @pl.when(i == 1)
-            def _():
-                tile_cp.wait_recv()
+            if tile_cp is not None:
+                @pl.when(i == 1)
+                def _():
+                    tile_cp.wait_recv()
 
             fn(pl.multiple_of(R * (2 * r + c + i * (1 - 2 * c)), R))
             return cy
@@ -286,40 +305,11 @@
         tile_cp.wait_send()
         combine(1, r, cp)
 
-    for l in range(L):
-        for r in range(2):
-            if l == 0:
-                if r == 0:
-                    for cp in (loc[0], wcopies[0][0]):
-                        cp.wait()
-                    tcp[0].wait()
-                    tcp[1].start()
-                src = lambda i, r=r: tokf[r, pl.ds(i, BLK), :].astype(F32) + emb_b[0:1, :]
-            else:
-                wait_y(1, r)
-                bd = vrow(5, l - 1)
-                src = lambda i, r=r, l=l, bd=bd: m_b[l - 1, r, pl.ds(i, BLK), :] + (ysum(1, r, i) + bd)
-            if r == 0 and l > 0:
-                wcopies[l][0].wait()
-            cp = enter_fwd(l, r, src, 0, h_b, a_b)
-            if r == 0:
-                wcopies[l][1].wait()
-            att_fwd(l, r, cp)
-        for r in range(2):
-            wait_y(0, r)
-            bo = vrow(2, l)
-            src = lambda i, r=r, l=l, bo=bo: h_b[l, r, pl.ds(i, BLK), :] + (ysum(0, r, i) + bo)
-            if r == 0:
-                wcopies[l][2].wait()
-                wcopies[l][3].wait()
-            cp = enter_fwd(l, r, src, 3, m_b, a2_b)
-            ffn_fwd(l, r, cp)
-
     def finish_output(r):
-        wait_y(1, r)
         bd = vrow(5, L - 1)
 
         def blk(i, cy):
+            wait_y(1, r, i)
             v = m_b[L - 1, r, pl.ds(i, BLK), :] + (ysum(1, r, i) + bd)
             tokf[r, pl.ds(i, BLK), :] = v.astype(BF)
             return cy
@@ -331,6 +321,7 @@
 
         def blk(i, cy):
             dg, db = cy
+            wait_y(par, r, i)
             x = xbuf[l, r, pl.ds(i, BLK), :]
             dy = ysum(par, r, i)
             xc, rstd = ln_stats(x)
@@ -357,25 +348,24 @@
         small[l, row : row + 1, :] = small[l, row : row + 1, :] + v
 
     def enter_b1(l, r):
+        cp = Tile(df_b, r, 2 + r if l == L - 1 else r)
         if l == L - 1:
             def blk(i, cy):
                 v = cotf[r, pl.ds(i, BLK), :]
                 dh_b[r, pl.ds(i, BLK), :] = v.astype(F32)
                 df_b[pl.ds(pl.multiple_of(own(r) + i, BLK), BLK), :] = v
+                cp.copy(i).start()
                 return cy
 
             rowloop(blk)
         else:
-            wait_y(0, r)
-
             def emit(i, dx):
                 v = dh_b[r, pl.ds(i, BLK), :] + dx
                 dh_b[r, pl.ds(i, BLK), :] = v
                 df_b[pl.ds(pl.multiple_of(own(r) + i, BLK), BLK), :] = v.astype(BF)
+                cp.copy(i).start()
 
             ln_bwd(l + 1, r, 0, 0, h_b, emit)
-        cp = tile_copy(df_b, r)
-        cp.start()
         colsum_own(df_b, r, l, 5)
         return cp
 
@@ -398,22 +388,24 @@
 
     def ffn_bwd(l, r, tile_cp):
         own_first(r, tile_cp, lambda q0: du_tile(l, q0))
+        if l == L - 1 and r == 1:
+            pl.semaphore_wait(turned, 1)
         cp = send_partner(r, lambda ref: da2_tile(l, oth(r), ref))
         da2_tile(l, own(r), part)
-        tile_cp.wait_send()
+        if tile_cp is not None:
+            tile_cp.wait_send()
         combine(2, r, cp)
 
     def enter_b2(l, r):
-        wait_y(2, r)
+        cp = Tile(dz_b, r)
 
         def emit(i, dx):
             v = dh_b[r, pl.ds(i, BLK), :] + dx
             dh_b[r, pl.ds(i, BLK), :] = v
             dz_b[pl.ds(pl.multiple_of(own(r) + i, BLK), BLK), :] = v.astype(BF)
+            cp.copy(i).start()
 
         ln_bwd(l, r, 2, 3, m_b, emit)
-        cp = tile_copy(dz_b, r)
-        cp.start()
         colsum_own(dz_b, r, l, 2)
         return cp
 
@@ -474,26 +466,26 @@
         tile_cp.wait_send()
         combine(0, r, cp)
 
-    WHOLE = (0, FL, None)
-    HALF = ((0, FL // 2, None), (FL // 2, FL - FL // 2, 3))
+    WHOLE = (0, FL, 0)
+    HALF = ((0, FL // 2, 0), (FL // 2, FL - FL // 2, 3))
 
     def r1_copy(j, k, span):
         c0, w, extra = span
-        q = j if extra is None else extra
+        q = j + extra
         peer = do_ * NI + lax.rem(di + k, NI)
         return dp_remote(send1.at[j, k - 1, :, c0 : c0 + w], recv1.at[j, k - 1, :, c0 : c0 + w],
                          r1s.at[q, k - 1], r1r.at[q, k - 1], peer)
 
     def r2_copy(j, k, span):
         c0, w, extra = span
-        q = j if extra is None else extra
+        q = j + extra
         peer = lax.rem(do_ + k, NO) * NI + di
         return dp_remote(send2.at[j, k - 1, :, c0 : c0 + w], recv2.at[j, k - 1, :, c0 : c0 + w],
                          r2s.at[q, k - 1], r2r.at[q, k - 1], peer)
 
     def g_copy(l, j, span):
         c0, w, extra = span
-        q = l * 3 + j if extra is None else 3 * L
+        q = l * 6 + j + extra
         return pltpu.make_async_copy(fstage.at[l, j, :, c0 : c0 + w], g_o.at[l, j, :, c0 : c0 + w], gsem.at[q])
 
     def piece(q):
@@ -548,12 +540,14 @@
         fstage[l, j, :, cols] = v
         g_copy(l, j, span).start()
 
-    def wgrad_ffn(l, j, lhs, rhs):
+    def wgrad_ffn(l, lhs, rhs, rows=slice(None), add=False):
         def one(n, cy):
             ns = pl.ds(pl.multiple_of(n * 256, 256), 256)
-            lt = lhs[:, ns].astype(F32).T.astype(BF)
+            lt = lhs[rows, ns].astype(F32).T.astype(BF)
             for f in range(FB):
-                gstage[ns, f * 256 : f * 256 + 256] = mm(lt, rhs[:, f * 256 : f * 256 + 256])
+                fs = slice(f * 256, f * 256 + 256)
+                v = mm(lt, rhs[rows, fs])
+                gstage[ns, fs] = gstage[ns, fs] + v if add else v
             return cy
 
         lax.fori_loop(0, NB, one, 0)
@@ -572,15 +566,51 @@
 
         lax.fori_loop(0, NB, one, 0)
 
-    loc[1].wait()
-    tcp[1].wait()
+    for l in range(L):
+        for r in range(2):
+            if l == 0:
+                if r == 0:
+                    for cp in (loc[0], wcopies[0][0]):
+                        cp.wait()
+                    tcp[0].wait()
+                    tcp[1].start()
+                src = lambda i, r=r: tokf[r, pl.ds(i, BLK), :].astype(F32) + emb_b[0:1, :]
+            else:
+                bd = vrow(5, l - 1)
+                src = lambda i, r=r, l=l, bd=bd: m_b[l - 1, r, pl.ds(i, BLK), :] + (ysum(1, r, i) + bd)
+            if r == 0 and l > 0:
+                wcopies[l][0].wait()
+            cp = enter_fwd(l, r, src, 0, h_b, a_b, 1 if l > 0 else None)
+            if r == 0:
+                wcopies[l][1].wait()
+            att_fwd(l, r, cp)
+        for r in range(2):
+            if l == L - 1 and r == 0:
+                loc[1].wait()
+                tcp[1].wait()
+                b1 = [enter_b1(l, 0), enter_b1(l, 1)]
+            elif l == L - 1:
+                b1[0].wait_recv()
+                wgrad_ffn(l, df_b, g_b.at[l], slice(0, CH))
+            bo = vrow(2, l)
+            src = lambda i, r=r, l=l, bo=bo: h_b[l, r, pl.ds(i, BLK), :] + (ysum(0, r, i) + bo)
+            if r == 0:
+                wcopies[l][2].wait()
+                wcopies[l][3].wait()
+            cp = enter_fwd(l, r, src, 3, m_b, a2_b, 0)
+            ffn_fwd(l, r, cp)
+
+    pl.semaphore_signal(turned, inc=1, device_id={"tensor": cpeer}, device_id_type=MESH)
+    b1[1].wait_recv()
+    wgrad_ffn(L - 1, df_b, g_b.at[L - 1], slice(CH, T), True)
+    rs_start(L - 1, 2)
+    for cp in b1:
+        cp.wait_send()
     for l in range(L - 1, -1, -1):
         last = l == L - 1
-        if last:
-            cps = {r: enter_b1(l, r) for r in (1, 0)}
+        spans = (WHOLE,) if l > 0 else HALF
         for r in (1, 0):
-            cp = cps[r] if last else enter_b1(l, r)
-            ffn_bwd(l, r, cp)
+            ffn_bwd(l, r, None if last else enter_b1(l, r))
             if not last:
                 rs_fin(l + 1, 1 + r)
         if last:
@@ -588,34 +618,38 @@
                 finish_output(r)
         else:
             rs_mid(l + 1, 0)
-        wgrad_ffn(l, 2, df_b, g_b.at[l])
-        rs_start(l, 2)
-        wgrad_ffn(l, 1, a2_b.at[l], gp_b.at[l])
-        rs_start(l, 1)
+            wgrad_ffn(l, df_b, g_b.at[l])
+            for span in spans:
+                rs_start(l, 2, span)
+        wgrad_ffn(l, a2_b.at[l], gp_b.at[l])
+        for span in spans:
+            rs_start(l, 1, span)
         dkv_acc[...] = jnp.zeros_like(dkv_acc)
         for r in (1, 0):
             cp = enter_b2(l, r)
+            if last and r == 1:
+                rs_mid(l, 2)
             att_bwd(l, r, cp)
-            if r == 1:
-                if not last:
-                    rs_fin(l + 1, 0)
-                rs_mid(l, 2)
-        if l > 0:
+            if not last and r == 1:
+                rs_fin(l + 1, 0)
+                for span in spans:
+                    rs_mid(l, 2, span)
+        if last:
+            rs_mid(l, 1)
             wgrad_att(l, WHOLE)
-            rs_mid(l, 1)
             rs_start(l, 0)
         else:
             wgrad_att(l, HALF[0])
-            rs_mid(l, 1)
+            rs_mid(l, 1, HALF[0])
             rs_start(l, 0, HALF[0])
             wgrad_att(l, HALF[1])
             rs_start(l, 0, HALF[1])
+            rs_mid(l, 1, HALF[1])
     ocp = pltpu.make_async_copy(tokf.at[y], out_o, osem.at[0])
     ocp.start()
-    rs_fin(0, 2)
+    for span in HALF:
+        rs_fin(0, 2, span)
     for r in (1, 0):
-        wait_y(0, r)
-
         def emit(i, dx, r=r):
             v = dh_b[r, pl.ds(i, BLK), :] + dx
             dh_b[r, pl.ds(i, BLK), :] = v
@@ -628,7 +662,6 @@
     gcp.start()
     scp = remote(small, smallr, ssem.at[0], ssem.at[1], cpeer)
     scp.start()
-    rs_fin(0, 1)
     scp.wait()
     shared = lax.broadcasted_iota(jnp.int32, (8, D), 0) < 7
     for l in range(L):
@@ -658,6 +691,8 @@
     for l, v in enumerate(columns(0)):
         smallx[d, l] = v
     rs_mid(0, 0, HALF[1])
+    for span in HALF:
+        rs_fin(0, 1, span)
     rs_fin(0, 0, HALF[0])
     lax.fori_loop(1, N, x_wait, 0)
     smallx_o[...] = smallx[...]
@@ -667,7 +702,7 @@
     if FUSED:
         for l in range(L):
             for j in range(3):
-                for span in HALF if l == 0 and j == 0 else (WHOLE,):
+                for span in HALF if l == 0 else (WHOLE,):
                     g_copy(l, j, span).wait()
 
 
@@ -735,7 +770,9 @@
     assert lax.axis_size("tensor") == 4 and ts.shape[0] == 1 and FL == D == 4 * HL and L > 1 and R == 256
     T = 4 * R
     W = -(-PER // 128) * 128
-    dim = dict(D=D, FL=FL, HL=HL, R=R, L=L, BLK=min(R, 128), W=W, N=N, NI=NI, NO=NO, PER=PER, FUSED=FUSED, TS=table.shape[0])
+    BLK = min(R, 128)
+    HB = R // BLK
+    dim = dict(D=D, FL=FL, HL=HL, R=R, L=L, BLK=BLK, W=W, N=N, NI=NI, NO=NO, PER=PER, FUSED=FUSED, TS=table.shape[0])
     vm = pl.BlockSpec(memory_space=pltpu.VMEM)
     sm = pl.BlockSpec(memory_space=pltpu.SMEM)
     any_ = pl.BlockSpec(memory_space=pl.ANY)
@@ -769,10 +806,10 @@
             V((L, 8, D), F32), V((L, 8, D), F32), V((N, L, 8, W), F32), V((N, L, 8, W), F32), V((8, D), F32),
             V((J, ones, NO * PR, FL), BF), V((J, ones, NO * PR, FL), BF), V((J, NO * PR, FL), F32),
             V((J, outs, PR, FL), BF), V((J, outs, PR, FL), BF), V((L, J, PR, FL), F32),
-            dma((L, 4)), dma((2,)), dma((2,)), dma((3, 2)), dma((3, 2)),
-            dma((2,)), dma((2,)), dma((2,)), dma((2,)),
-            dma((3,)), dma((2,)), dma((3 * L + 1,)), dma((2,)), dma((N,)), dma((N,)),
-            dma((4, ones)), dma((4, ones)), dma((4, outs)), dma((4, outs)),
+            dma((L, 4)), dma((2,)), dma((2,)), dma((3, 2, HB)), dma((3, 2, HB)),
+            dma((4, HB)), dma((4, HB)), dma((2,)), dma((2,)),
+            dma((3,)), dma((2,)), dma((6 * L,)), dma((2,)), dma((N,)), dma((N,)),
+            dma((6, ones)), dma((6, ones)), dma((6, outs)), dma((6, outs)), pltpu.SemaphoreType.REGULAR,
         ],
         compiler_params=pltpu.CompilerParams(
             collective_id=0, has_side_effects=True, vmem_limit_bytes=67043328),

time: 207 us -> 201 us (0.971)
  Pallas kernels: 204 us -> 198 us
    pallas_call x1, Pallas kernels: 200 us -> 193 us  [run_step(): pl.pallas_call(functools.partial(step_kernel, dim), out_shape=(jax.ShapeD...]
where the time goes in v1:
time: 201 us; the launch traced here: 200 us
  Pallas kernels  198 us (99%)
  between operations  2.13 us (1%)
    pallas_call x1, Pallas kernels, run_step(): pl.pallas_call(functools.partial(step_kernel, dim), out_shape=(jax.ShapeD...  193 us
    pallas_call x1, Pallas kernels, local(): pl.pallas_call(functools.partial(finish_kernel, dim), out_shape=(jax.Shap...  4.67 us

profile of v1, /device:TPU:0, one launch (start us, length us, event | category | flops | bytes accessed | tf_op | source)
XLA Modules:
  0.0 200.3 jit_solution(11969379137282654702)
XLA Ops:
  1.9 193.5 %layers.1 = (bf16[256,768]{1,0:T(8,128)(2,1)}, f32[256,768]{1,0:T(8,128)}, f32[8,2,8,128]{3,2,1,0:T(8,128)}, f32[2,3,96,768]{3,2,1,0:T(8,128)}) custom-call(s32[1]{0:T(128)S(6)} %copy.30.refs_0_, s32[1]{0:T(128)S(6)} %copy.31.refs_1_, bf16[2,768]{1,0:T(2,128)(2,1)} %refs_2_.1, bf16[2,768]{1,0:T(2,128)(2,1)} %refs_3_.1, bf16[2,768]{1,0:T(2,128)(2,1)} %refs_4_.1, ...), custom_call_target="tpu_custom_call" | custom-call | tf_op jit(solution)/shard_map/layers/pallas_call | solution.py:786
  195.4 4.7 %finish.1 = (bf16[256,768]{1,0:T(8,128)(2,1)}, f32[256,768]{1,0:T(8,128)}, f32[96,1000]{1,0:T(8,128)}, f32[2,96]{1,0:T(2,128)}, f32[2,96]{1,0:T(2,128)}, /*index...) custom-call(bf16[256,768]{1,0:T(8,128)(2,1)} %get-tuple-element.32.o, ...), custom_call_target="tpu_custom_call" | custom-call | tf_op jit(solution)/shard_map/finish/pallas_call | solution.py:835

commit v2 on v1

--- a/solution.py
+++ b/solution.py
@@ -61,6 +61,7 @@
     c = lax.rem(t, 2)
     ypeer = lax.rem(t + 2, 4)
     cpeer = t + 1 - 2 * c
+    dpeer = lax.rem(cpeer + 2, 4)
 
     def own(r):
         return pl.multiple_of(R * (2 * r + c), R)
@@ -87,6 +88,7 @@
     lax.fori_loop(1, N, greet, 0)
     pl.semaphore_signal(bar, inc=1, device_id={"tensor": ypeer}, device_id_type=MESH)
     pl.semaphore_signal(bar, inc=1, device_id={"tensor": cpeer}, device_id_type=MESH)
+    pl.semaphore_signal(bar, inc=1, device_id={"tensor": dpeer}, device_id_type=MESH)
 
     loc = [pltpu.make_async_copy(tok_in, tokf.at[y], lsem.at[0]),
            pltpu.make_async_copy(cot_in, cotf.at[y], lsem.at[1]),
@@ -101,7 +103,7 @@
             cp.start()
             row.append(cp)
         wcopies.append(row)
-    pl.semaphore_wait(bar, N + 1)
+    pl.semaphore_wait(bar, N + 2)
     tcp = [remote(tok_in, tokf.at[y], tsem_s.at[0], tsem_r.at[0], ypeer),
            remote(cot_in, cotf.at[y], tsem_s.at[1], tsem_r.at[1], ypeer)]
     tcp[0].start()
@@ -175,19 +177,28 @@
         cp.wait_send()
         cp.wait_recv()
 
+    def wait_mine(par, i):
+        y_copy(par, 1 - y, i).wait_send()
+        y_copy(par, y, i).wait_recv()
+
     def send_partner(r, fill):
         fill(csend.at[r])
         cp = part_copy(r)
         cp.start()
         return cp
 
-    def combine(par, r, cp):
+    def combine(par, r, cp, last=False):
         cp.wait_recv()
 
         def blk(i, cy):
             v = part[pl.ds(i, BLK), :] + crecv[r, pl.ds(i, BLK), :].astype(F32)
             ysend[par, r, pl.ds(i, BLK), :] = v.astype(BF)
-            y_copy(par, r, i).start()
+            if last:
+                @pl.when(y == 1 - r)
+                def _():
+                    y_copy(par, r, i).start()
+            else:
+                y_copy(par, r, i).start()
             return cy
 
         rowloop(blk)
@@ -303,25 +314,28 @@
         cp = send_partner(r, lambda ref: down_tile(l, oth(r), ref))
         down_tile(l, own(r), part)
         tile_cp.wait_send()
-        combine(1, r, cp)
-
-    def finish_output(r):
+        combine(1, r, cp, l == L - 1)
+
+    def finish_output():
         bd = vrow(5, L - 1)
 
         def blk(i, cy):
-            wait_y(1, r, i)
-            v = m_b[L - 1, r, pl.ds(i, BLK), :] + (ysum(1, r, i) + bd)
-            tokf[r, pl.ds(i, BLK), :] = v.astype(BF)
+            wait_mine(1, i)
+            v = m_b[L - 1, y, pl.ds(i, BLK), :] + (ysum(1, y, i) + bd)
+            tokf[y, pl.ds(i, BLK), :] = v.astype(BF)
             return cy
 
         rowloop(blk)
 
-    def ln_bwd(l, r, par, gi, xbuf, emit):
+    def ln_bwd(l, r, par, gi, xbuf, emit, mine=False):
         gain = vrow(gi, l)
 
         def blk(i, cy):
             dg, db = cy
-            wait_y(par, r, i)
+            if mine:
+                wait_mine(par, i)
+            else:
+                wait_y(par, r, i)
             x = xbuf[l, r, pl.ds(i, BLK), :]
             dy = ysum(par, r, i)
             xc, rstd = ln_stats(x)
@@ -464,7 +478,7 @@
         cp = send_partner(r, lambda ref: da_tile(l, oth(r), ref))
         da_tile(l, own(r), part)
         tile_cp.wait_send()
-        combine(0, r, cp)
+        combine(0, r, cp, l == 0)
 
     WHOLE = (0, FL, 0)
     HALF = ((0, FL // 2, 0), (FL // 2, FL - FL // 2, 3))
@@ -614,8 +628,7 @@
             if not last:
                 rs_fin(l + 1, 1 + r)
         if last:
-            for r in (1, 0):
-                finish_output(r)
+            finish_output()
         else:
             rs_mid(l + 1, 0)
             wgrad_ffn(l, df_b, g_b.at[l])
@@ -649,23 +662,27 @@
     ocp.start()
     for span in HALF:
         rs_fin(0, 2, span)
-    for r in (1, 0):
-        def emit(i, dx, r=r):
-            v = dh_b[r, pl.ds(i, BLK), :] + dx
-            dh_b[r, pl.ds(i, BLK), :] = v
-            small[0, 6:7, :] = small[0, 6:7, :] + jnp.sum(v, axis=0, keepdims=True)
-
-        ln_bwd(0, r, 0, 0, h_b, emit)
-        if r == 1:
-            rs_mid(0, 0, HALF[0])
+    rs_mid(0, 0, HALF[0])
+
+    def emit(i, dx):
+        v = dh_b[y, pl.ds(i, BLK), :] + dx
+        dh_b[y, pl.ds(i, BLK), :] = v
+        small[0, 6:7, :] = small[0, 6:7, :] + jnp.sum(v, axis=0, keepdims=True)
+
+    ln_bwd(0, y, 0, 0, h_b, emit, True)
     gcp = pltpu.make_async_copy(dh_b.at[y], gtok_o, osem.at[1])
     gcp.start()
-    scp = remote(small, smallr, ssem.at[0], ssem.at[1], cpeer)
-    scp.start()
-    scp.wait()
-    shared = lax.broadcasted_iota(jnp.int32, (8, D), 0) < 7
+    scps = [remote(small, smallr.at[0:L], ssem.at[0], ssem.at[3], cpeer),
+            remote(small.at[0], smallr.at[L], ssem.at[1], ssem.at[4], ypeer),
+            remote(small.at[0], smallr.at[L + 1], ssem.at[2], ssem.at[5], dpeer)]
+    for scp in scps:
+        scp.start()
+    for scp in scps:
+        scp.wait()
+    which = lax.broadcasted_iota(jnp.int32, (8, D), 0)
+    small[0] = small[0] + jnp.where((which < 2) | (which == 6), smallr[L] + smallr[L + 1], 0.0)
     for l in range(L):
-        small[l] = small[l] + jnp.where(shared, smallr[l], 0.0)
+        small[l] = small[l] + jnp.where(which < 7, smallr[l], 0.0)
     small[1, 6:7, :] = jnp.full((1, D), ts_ref[0].astype(F32), F32)
 
     def x_copy(k):
@@ -803,12 +820,12 @@
             V((HL, T), BF), V((3 * HL, T), BF), V((2, HL, T), F32),
             V((3, 2, R, D), BF), V((3, 2, R, D), BF), V((2, R, D), BF), V((2, R, D), BF),
             V((R, D), F32), V((T, R), F32), V((T, R), BF), V((T, R), BF), V((D, FL), F32),
-            V((L, 8, D), F32), V((L, 8, D), F32), V((N, L, 8, W), F32), V((N, L, 8, W), F32), V((8, D), F32),
+            V((L, 8, D), F32), V((L + 2, 8, D), F32), V((N, L, 8, W), F32), V((N, L, 8, W), F32), V((8, D), F32),
             V((J, ones, NO * PR, FL), BF), V((J, ones, NO * PR, FL), BF), V((J, NO * PR, FL), F32),
             V((J, outs, PR, FL), BF), V((J, outs, PR, FL), BF), V((L, J, PR, FL), F32),
             dma((L, 4)), dma((2,)), dma((2,)), dma((3, 2, HB)), dma((3, 2, HB)),
             dma((4, HB)), dma((4, HB)), dma((2,)), dma((2,)),
-            dma((3,)), dma((2,)), dma((6 * L,)), dma((2,)), dma((N,)), dma((N,)),
+            dma((3,)), dma((2,)), dma((6 * L,)), dma((6,)), dma((N,)), dma((N,)),
             dma((6, ones)), dma((6, ones)), dma((6, outs)), dma((6, outs)), pltpu.SemaphoreType.REGULAR,
         ],
         compiler_params=pltpu.CompilerParams(

time: 201 us -> 199 us (0.990)
  no operation moved by 1% of the time
where the time goes in v2:
time: 199 us
  Pallas kernels  197 us (99%)
  between operations  2.13 us (1%)
    pallas_call x1, Pallas kernels, run_step(): pl.pallas_call(functools.partial(step_kernel, dim), out_shape=(jax.ShapeD...  192 us
    pallas_call x1, Pallas kernels, local(): pl.pallas_call(functools.partial(finish_kernel, dim), out_shape=(jax.Shap...  4.67 us

profile of v2, /device:TPU:0, one launch (start us, length us, event | category | flops | bytes accessed | tf_op | source)
XLA Modules:
  0.0 198.9 jit_solution(18226926280544755304)
XLA Ops:
  1.9 192.1 %layers.1 = (bf16[256,768]{1,0:T(8,128)(2,1)}, f32[256,768]{1,0:T(8,128)}, f32[8,2,8,128]{3,2,1,0:T(8,128)}, f32[2,3,96,768]{3,2,1,0:T(8,128)}) custom-call(s32[1]{0:T(128)S(6)} %copy.30.refs_0_, s32[1]{0:T(128)S(6)} %copy.31.refs_1_, bf16[2,768]{1,0:T(2,128)(2,1)} %refs_2_.1, bf16[2,768]{1,0:T(2,128)(2,1)} %refs_3_.1, bf16[2,768]{1,0:T(2,128)(2,1)} %refs_4_.1, ...), custom_call_target="tpu_custom_call" | custom-call | tf_op jit(solution)/shard_map/layers/pallas_call | solution.py:803
  194.1 4.7 %finish.1 = (bf16[256,768]{1,0:T(8,128)(2,1)}, f32[256,768]{1,0:T(8,128)}, f32[96,1000]{1,0:T(8,128)}, f32[2,96]{1,0:T(2,128)}, f32[2,96]{1,0:T(2,128)}, /*index...) custom-call(bf16[256,768]{1,0:T(8,128)(2,1)} %get-tuple-element.32.o, ...), custom_call_target="tpu_custom_call" | custom-call | tf_op jit(solution)/shard_map/finish/pallas_call | solution.py:852

commit v3 on v2

--- a/solution.py
+++ b/solution.py
@@ -278,12 +278,14 @@
 
         nblocks(one, NB)
 
-    def own_first(r, tile_cp, fn):
+    def own_first(r, tile_cp, fn, between=None):
         def tile(i, cy):
             if tile_cp is not None:
                 @pl.when(i == 1)
                 def _():
                     tile_cp.wait_recv()
+                    if between is not None:
+                        between()
 
             fn(pl.multiple_of(R * (2 * r + c + i * (1 - 2 * c)), R))
             return cy
@@ -466,12 +468,12 @@
 
         nblocks(one, NB)
 
-    def att_bwd(l, r, tile_cp):
+    def att_bwd(l, r, tile_cp, between=None):
         def both(q0):
             do_tile(l, q0)
             att_bwd_tile(l, r, q0)
 
-        own_first(r, tile_cp, both)
+        own_first(r, tile_cp, both, between)
         cs = slice(CH * r, CH * r + CH)
         for j in range(2):
             dqT_b[HP * (j + 1) : HP * (j + 1) + HL, cs] = dkv_acc[j, 0:HL, cs].astype(BF)
@@ -482,6 +484,7 @@
 
     WHOLE = (0, FL, 0)
     HALF = ((0, FL // 2, 0), (FL // 2, FL - FL // 2, 3))
+    THIRD = tuple((i * 256, 256, 3 * i) for i in range(FL // 256))
 
     def r1_copy(j, k, span):
         c0, w, extra = span
@@ -499,7 +502,7 @@
 
     def g_copy(l, j, span):
         c0, w, extra = span
-        q = l * 6 + j + extra
+        q = l * 9 + j + extra
         return pltpu.make_async_copy(fstage.at[l, j, :, c0 : c0 + w], g_o.at[l, j, :, c0 : c0 + w], gsem.at[q])
 
     def piece(q):
@@ -620,49 +623,49 @@
     rs_start(L - 1, 2)
     for cp in b1:
         cp.wait_send()
+    def many(fn, l, j, spans):
+        for span in spans:
+            fn(l, j, span)
+
     for l in range(L - 1, -1, -1):
         last = l == L - 1
-        spans = (WHOLE,) if l > 0 else HALF
-        for r in (1, 0):
-            ffn_bwd(l, r, None if last else enter_b1(l, r))
-            if not last:
-                rs_fin(l + 1, 1 + r)
+        spans = (WHOLE,) if last else HALF
+        ends = HALF if l > 0 else THIRD
         if last:
+            for r in (1, 0):
+                ffn_bwd(l, r, None)
             finish_output()
         else:
-            rs_mid(l + 1, 0)
+            ffn_bwd(l, 1, enter_b1(l, 1))
+            many(rs_fin, l + 1, 2, (WHOLE,) if l + 1 == L - 1 else HALF)
+            rs_mid(l + 1, 0, HALF[0])
+            cp = enter_b1(l, 0)
+            cp.wait_recv()
             wgrad_ffn(l, df_b, g_b.at[l])
-            for span in spans:
-                rs_start(l, 2, span)
+            many(rs_start, l, 2, spans)
+            cp.wait_send()
+            many(rs_fin, l + 1, 1, (WHOLE,) if l + 1 == L - 1 else HALF)
+            rs_mid(l + 1, 0, HALF[1])
+            ffn_bwd(l, 0, None)
         wgrad_ffn(l, a2_b.at[l], gp_b.at[l])
-        for span in spans:
-            rs_start(l, 1, span)
+        many(rs_start, l, 1, spans)
         dkv_acc[...] = jnp.zeros_like(dkv_acc)
-        for r in (1, 0):
-            cp = enter_b2(l, r)
-            if last and r == 1:
-                rs_mid(l, 2)
-            att_bwd(l, r, cp)
-            if not last and r == 1:
-                rs_fin(l + 1, 0)
-                for span in spans:
-                    rs_mid(l, 2, span)
-        if last:
-            rs_mid(l, 1)
-            wgrad_att(l, WHOLE)
-            rs_start(l, 0)
-        else:
-            wgrad_att(l, HALF[0])
-            rs_mid(l, 1, HALF[0])
-            rs_start(l, 0, HALF[0])
-            wgrad_att(l, HALF[1])
-            rs_start(l, 0, HALF[1])
-            rs_mid(l, 1, HALF[1])
+        cp = enter_b2(l, 1)
+        if not last:
+            many(rs_fin, l + 1, 0, HALF)
+        rs_mid(l, 2, spans[0])
+        att_bwd(l, 1, cp, None if last else lambda l=l, span=HALF[1]: rs_mid(l, 2, span))
+        cp = enter_b2(l, 0)
+        att_bwd(l, 0, cp, lambda l=l, span=spans[0]: rs_mid(l, 1, span))
+        for i, span in enumerate(ends):
+            wgrad_att(l, span)
+            if not last and i == 1:
+                rs_mid(l, 1, HALF[1])
+            rs_start(l, 0, span)
     ocp = pltpu.make_async_copy(tokf.at[y], out_o, osem.at[0])
     ocp.start()
-    for span in HALF:
-        rs_fin(0, 2, span)
-    rs_mid(0, 0, HALF[0])
+    many(rs_fin, 0, 2, HALF)
+    rs_mid(0, 0, THIRD[0])
 
     def emit(i, dx):
         v = dh_b[y, pl.ds(i, BLK), :] + dx
@@ -677,6 +680,7 @@
             remote(small.at[0], smallr.at[L + 1], ssem.at[2], ssem.at[5], dpeer)]
     for scp in scps:
         scp.start()
+    many(rs_mid, 0, 0, THIRD[1:])
     for scp in scps:
         scp.wait()
     which = lax.broadcasted_iota(jnp.int32, (8, D), 0)
@@ -707,19 +711,17 @@
     lax.fori_loop(1, N, x_go, 0)
     for l, v in enumerate(columns(0)):
         smallx[d, l] = v
-    rs_mid(0, 0, HALF[1])
-    for span in HALF:
-        rs_fin(0, 1, span)
-    rs_fin(0, 0, HALF[0])
+    many(rs_fin, 0, 1, HALF)
+    many(rs_fin, 0, 0, THIRD[:-1])
     lax.fori_loop(1, N, x_wait, 0)
     smallx_o[...] = smallx[...]
-    rs_fin(0, 0, HALF[1])
+    rs_fin(0, 0, THIRD[-1])
     ocp.wait()
     gcp.wait()
     if FUSED:
         for l in range(L):
             for j in range(3):
-                for span in HALF if l == 0 else (WHOLE,):
+                for span in THIRD if l == 0 and j == 0 else HALF if l < L - 1 or j == 0 else (WHOLE,):
                     g_copy(l, j, span).wait()
 
 
@@ -784,7 +786,7 @@
     NI, NO = split_of(N)
     PER = D // N
     FUSED = PER % 16 == 0
-    assert lax.axis_size("tensor") == 4 and ts.shape[0] == 1 and FL == D == 4 * HL and L > 1 and R == 256
+    assert lax.axis_size("tensor") == 4 and ts.shape[0] == 1 and FL == D == 4 * HL and L > 1 and R == 256 and FL == 768
     T = 4 * R
     W = -(-PER // 128) * 128
     BLK = min(R, 128)
@@ -825,8 +827,8 @@
             V((J, outs, PR, FL), BF), V((J, outs, PR, FL), BF), V((L, J, PR, FL), F32),
             dma((L, 4)), dma((2,)), dma((2,)), dma((3, 2, HB)), dma((3, 2, HB)),
             dma((4, HB)), dma((4, HB)), dma((2,)), dma((2,)),
-            dma((3,)), dma((2,)), dma((6 * L,)), dma((6,)), dma((N,)), dma((N,)),
-            dma((6, ones)), dma((6, ones)), dma((6, outs)), dma((6, outs)), pltpu.SemaphoreType.REGULAR,
+            dma((3,)), dma((2,)), dma((9 * L,)), dma((6,)), dma((N,)), dma((N,)),
+            dma((9, ones)), dma((9, ones)), dma((9, outs)), dma((9, outs)), pltpu.SemaphoreType.REGULAR,
         ],
         compiler_params=pltpu.CompilerParams(
             collective_id=0, has_side_effects=True, vmem_limit_bytes=67043328),

time: 199 us -> 195 us (0.980)
  Pallas kernels: 197 us -> 192 us
    pallas_call x1, Pallas kernels: 192 us -> 188 us  [run_step(): pl.pallas_call(functools.partial(step_kernel, dim), out_shape=(jax.ShapeD...]
where the time goes in v3:
time: 195 us
  Pallas kernels  192 us (98%)
  between operations  2.13 us (1%)
    pallas_call x1, Pallas kernels, run_step(): pl.pallas_call(functools.partial(step_kernel, dim), out_shape=(jax.ShapeD...  188 us
    pallas_call x1, Pallas kernels, local(): pl.pallas_call(functools.partial(finish_kernel, dim), out_shape=(jax.Shap...  4.67 us

profile of v3, /device:TPU:0, one launch (start us, length us, event | category | flops | bytes accessed | tf_op | source)
XLA Modules:
  0.0 194.6 jit_solution(2748628812152192878)
XLA Ops:
  1.9 187.8 %layers.1 = (bf16[256,768]{1,0:T(8,128)(2,1)}, f32[256,768]{1,0:T(8,128)}, f32[8,2,8,128]{3,2,1,0:T(8,128)}, f32[2,3,96,768]{3,2,1,0:T(8,128)}) custom-call(s32[1]{0:T(128)S(6)} %copy.30.refs_0_, s32[1]{0:T(128)S(6)} %copy.31.refs_1_, bf16[2,768]{1,0:T(2,128)(2,1)} %refs_2_.1, bf16[2,768]{1,0:T(2,128)(2,1)} %refs_3_.1, bf16[2,768]{1,0:T(2,128)(2,1)} %refs_4_.1, ...), custom_call_target="tpu_custom_call" | custom-call | tf_op jit(solution)/shard_map/layers/pallas_call | solution.py:805
  189.7 4.7 %finish.1 = (bf16[256,768]{1,0:T(8,128)(2,1)}, f32[256,768]{1,0:T(8,128)}, f32[96,1000]{1,0:T(8,128)}, f32[2,96]{1,0:T(2,128)}, f32[2,96]{1,0:T(2,128)}, /*index...) custom-call(bf16[256,768]{1,0:T(8,128)(2,1)} %get-tuple-element.32.o, ...), custom_call_target="tpu_custom_call" | custom-call | tf_op jit(solution)/shard_map/finish/pallas_call | solution.py:854

commit v4 on v3

--- a/solution.py
+++ b/solution.py
@@ -218,7 +218,7 @@
 
     def visible(r, kb, q0):
         key = lax.broadcasted_iota(jnp.int32, (R, R), 0) + (CH * r + kb * R)
-        qry = lax.broadcasted_iota(jnp.int32, (R, R), 1) + q0
+        qry = lax.broadcasted_iota(jnp.int32, (1, R), 1) + q0
         return key <= (qry | (bs - 1))
 
     def att_fwd_tile(l, r, q0):
@@ -485,6 +485,7 @@
     WHOLE = (0, FL, 0)
     HALF = ((0, FL // 2, 0), (FL // 2, FL - FL // 2, 3))
     THIRD = tuple((i * 256, 256, 3 * i) for i in range(FL // 256))
+    PARTS = THIRD[:2] + ((512, 128, 6), (640, 128, 9))
 
     def r1_copy(j, k, span):
         c0, w, extra = span
@@ -502,7 +503,7 @@
 
     def g_copy(l, j, span):
         c0, w, extra = span
-        q = l * 9 + j + extra
+        q = l * 12 + j + extra
         return pltpu.make_async_copy(fstage.at[l, j, :, c0 : c0 + w], g_o.at[l, j, :, c0 : c0 + w], gsem.at[q])
 
     def piece(q):
@@ -659,13 +660,13 @@
         att_bwd(l, 0, cp, lambda l=l, span=spans[0]: rs_mid(l, 1, span))
         for i, span in enumerate(ends):
             wgrad_att(l, span)
-            if not last and i == 1:
+            if not last and i == 0:
                 rs_mid(l, 1, HALF[1])
-            rs_start(l, 0, span)
+            many(rs_start, l, 0, PARTS[2:] if not last and i == 2 else (span,))
     ocp = pltpu.make_async_copy(tokf.at[y], out_o, osem.at[0])
     ocp.start()
     many(rs_fin, 0, 2, HALF)
-    rs_mid(0, 0, THIRD[0])
+    rs_mid(0, 0, PARTS[0])
 
     def emit(i, dx):
         v = dh_b[y, pl.ds(i, BLK), :] + dx
@@ -680,7 +681,7 @@
             remote(small.at[0], smallr.at[L + 1], ssem.at[2], ssem.at[5], dpeer)]
     for scp in scps:
         scp.start()
-    many(rs_mid, 0, 0, THIRD[1:])
+    many(rs_mid, 0, 0, PARTS[1:])
     for scp in scps:
         scp.wait()
     which = lax.broadcasted_iota(jnp.int32, (8, D), 0)
@@ -712,16 +713,16 @@
     for l, v in enumerate(columns(0)):
         smallx[d, l] = v
     many(rs_fin, 0, 1, HALF)
-    many(rs_fin, 0, 0, THIRD[:-1])
+    many(rs_fin, 0, 0, PARTS[:-1])
     lax.fori_loop(1, N, x_wait, 0)
     smallx_o[...] = smallx[...]
-    rs_fin(0, 0, THIRD[-1])
+    rs_fin(0, 0, PARTS[-1])
     ocp.wait()
     gcp.wait()
     if FUSED:
         for l in range(L):
             for j in range(3):
-                for span in THIRD if l == 0 and j == 0 else HALF if l < L - 1 or j == 0 else (WHOLE,):
+                for span in PARTS if l == 0 and j == 0 else HALF if l < L - 1 or j == 0 else (WHOLE,):
                     g_copy(l, j, span).wait()
 
 
@@ -827,8 +828,8 @@
             V((J, outs, PR, FL), BF), V((J, outs, PR, FL), BF), V((L, J, PR, FL), F32),
             dma((L, 4)), dma((2,)), dma((2,)), dma((3, 2, HB)), dma((3, 2, HB)),
             dma((4, HB)), dma((4, HB)), dma((2,)), dma((2,)),
-            dma((3,)), dma((2,)), dma((9 * L,)), dma((6,)), dma((N,)), dma((N,)),
-            dma((9, ones)), dma((9, ones)), dma((9, outs)), dma((9, outs)), pltpu.SemaphoreType.REGULAR,
+            dma((3,)), dma((2,)), dma((12 * L,)), dma((6,)), dma((N,)), dma((N,)),
+            dma((12, ones)), dma((12, ones)), dma((12, outs)), dma((12, outs)), pltpu.SemaphoreType.REGULAR,
         ],
         compiler_params=pltpu.CompilerParams(
             collective_id=0, has_side_effects=True, vmem_limit_bytes=67043328),

time: 195 us -> 195 us (level)
  no operation moved by 1% of the time
where the time goes in v4:
time: 195 us
  Pallas kernels  193 us (99%)
  between operations  2.13 us (1%)
    pallas_call x1, Pallas kernels, run_step(): pl.pallas_call(functools.partial(step_kernel, dim), out_shape=(jax.ShapeD...  188 us
    pallas_call x1, Pallas kernels, local(): pl.pallas_call(functools.partial(finish_kernel, dim), out_shape=(jax.Shap...  4.67 us

profile of v4, /device:TPU:0, one launch (start us, length us, event | category | flops | bytes accessed | tf_op | source)
XLA Modules:
  0.0 194.7 jit_solution(3149337200316777681)
XLA Ops:
  1.9 187.9 %layers.1 = (bf16[256,768]{1,0:T(8,128)(2,1)}, f32[256,768]{1,0:T(8,128)}, f32[8,2,8,128]{3,2,1,0:T(8,128)}, f32[2,3,96,768]{3,2,1,0:T(8,128)}) custom-call(s32[1]{0:T(128)S(6)} %copy.30.refs_0_, s32[1]{0:T(128)S(6)} %copy.31.refs_1_, bf16[2,768]{1,0:T(2,128)(2,1)} %refs_2_.1, bf16[2,768]{1,0:T(2,128)(2,1)} %refs_3_.1, bf16[2,768]{1,0:T(2,128)(2,1)} %refs_4_.1, ...), custom_call_target="tpu_custom_call" | custom-call | tf_op jit(solution)/shard_map/layers/pallas_call | solution.py:806
  189.9 4.7 %finish.1 = (bf16[256,768]{1,0:T(8,128)(2,1)}, f32[256,768]{1,0:T(8,128)}, f32[96,1000]{1,0:T(8,128)}, f32[2,96]{1,0:T(2,128)}, f32[2,96]{1,0:T(2,128)}, /*index...) custom-call(bf16[256,768]{1,0:T(8,128)(2,1)} %get-tuple-element.32.o, ...), custom_call_target="tpu_custom_call" | custom-call | tf_op jit(solution)/shard_map/finish/pallas_call | solution.py:855
